TPU v7x, 256 devices: a whole 4x4x8 slice. The times are simulated.
256 devices in a mesh: seq: 16 (over y, x), exp: 16 (over z, core).
Axes of the slice: x: 4, y: 4, z: 8, core: 2. Of those that a mesh axis runs over, the one named last changes fastest.
Arguments:
- x_in: bfloat16 [4096, 8192], P('seq', 'exp'), may hold values from -6 to 6
- z_gate: bfloat16 [4096, 8192], P('seq', 'exp'), may hold values from -6 to 6
- b_in: bfloat16 [4096, 128], P('seq'), may hold values from -0.52734375 to 0.52734375
- c_out: bfloat16 [4096, 128], P('seq'), may hold values from -0.1875 to 0.1875
- dt_step: float32 [4096, 128], P('seq', 'exp'), may hold values from 0.12 to 2052, as said below
- rate: float32 [128], P('exp'), may hold values from 0 to 0.06, as said below
- skip: float32 [128], P('exp'), may hold values from 0.5 to 1.5
- init_state: float32 [128, 64, 128], P('exp'), may hold values from -16.970562 to 16.970562
- residual: bfloat16 [4096, 8192], P(('seq', 'exp')), may hold values from -6 to 6
- norm_gain: float32 [8192], replicated, may hold values from 0.5 to 1.5
- expert_ids: int32 [4096, 2], P(('seq', 'exp')), may hold values from 0 to 15, all different within a row; in each aligned block of 16 rows (0 to 15, 16 to 31, ...) at most 3 rows name the same one
- gate_weights: float32 [4096, 2], P(('seq', 'exp')), may hold values from 0.2 to 1
- w_gate: bfloat16 [16, 8192, 2048], P('exp', None, 'seq'), may hold values from -0.0625 to 0.0625
- w_up: bfloat16 [16, 8192, 2048], P('exp', None, 'seq'), may hold values from -0.0625 to 0.0625
- w_down: bfloat16 [16, 2048, 8192], P('exp', 'seq'), may hold values from -0.125 to 0.125
Outputs:
- layer_out: bfloat16 [4096, 8192], P(('seq', 'exp'))
Inputs may be any that keep to these rules, and one draw needn't show every extreme that they name: `dt_step`: positive step sizes. `rate`: positive rates. `expert_ids`: each row names two different experts; among the rows of one device (aligned blocks of 16 rows) no expert is named by more than 3 rows, and in every draw some expert is named by exactly 3 rows of some block.
All inputs are finite; a program needn't handle non-finite values.
Results may differ from a plain program's by a relative error of at most 0.0095.
Values may be sent and summed in bfloat16 or wider, within the bound.
A program may use at most 128 MiB of HBM per device.

v0:
```python
import jax
import jax.numpy as jnp
from jax import lax
from jax.sharding import PartitionSpec as P

GROUP = 128
PRECISE = lax.Precision.HIGHEST


def exclusive_scan(log, state, axis):
    devices = lax.axis_size(axis)
    inc = (log, state)
    exc = (jnp.zeros_like(log), jnp.zeros_like(state))
    shift = 1
    while shift < devices:
        pairs = [(i, i + shift) for i in range(devices - shift)]
        got = (lax.ppermute(inc[0], axis, pairs), lax.ppermute(inc[1], axis, pairs))
        exc = chain_combine(got, exc)
        inc = chain_combine(got, inc)
        shift *= 2
    return exc


def chain_combine(earlier, later):
    return (earlier[0] + later[0], jnp.exp(later[0])[:, None, None] * earlier[1] + later[1])


def on_device(
    x_in,
    z_gate,
    b_in,
    c_out,
    dt_step,
    rate,
    skip,
    init_state,
    residual,
    norm_gain,
    expert_ids,
    gate_weights,
    w_gate,
    w_up,
    w_down,
):
    token_count, channels = x_in.shape
    heads_here = rate.shape[0]
    head_width = channels // heads_here
    state_width = b_in.shape[1]
    blocks = token_count // GROUP
    inputs = x_in.astype(jnp.float32).reshape(blocks, GROUP, heads_here, head_width)
    keys_in = b_in.astype(jnp.float32).reshape(blocks, GROUP, state_width)
    queries = c_out.astype(jnp.float32).reshape(blocks, GROUP, state_width)
    log_steps = (-rate[None, :] * dt_step).reshape(blocks, GROUP, heads_here)
    cumulative = jnp.cumsum(log_steps, axis=1)
    scores = jnp.einsum("ctn,csn->cts", queries, keys_in, precision=PRECISE)
    causal = jnp.arange(GROUP)[:, None] >= jnp.arange(GROUP)[None, :]
    spread = cumulative[:, :, None, :] - cumulative[:, None, :, :]
    weights = jnp.exp(jnp.where(causal[None, :, :, None], spread, -jnp.inf)) * scores[..., None]
    intra_out = jnp.einsum("ctsh,cshp->cthp", weights, inputs, precision=PRECISE)
    tail_decay = jnp.exp(cumulative[:, -1:, :] - cumulative)
    block_state = jnp.einsum("csh,cshp,csn->chpn", tail_decay, inputs, keys_in, precision=PRECISE)
    block_log = cumulative[:, -1, :]

    def advance(carried, element):
        total_log, total_state = carried
        step_log, step_state = element
        updated = (
            total_log + step_log,
            jnp.exp(step_log)[:, None, None] * total_state + step_state,
        )
        return (updated, (total_log, total_state))

    zero_state = jnp.zeros((heads_here, head_width, state_width), jnp.float32)
    zero_log = jnp.zeros((heads_here,), jnp.float32)
    (device_log, device_state), (enter_log, enter_state) = lax.scan(
        advance, (zero_log, zero_state), (block_log, block_state)
    )
    prior_log, prior_state = exclusive_scan(device_log, device_state, "seq")
    incoming = prior_state + jnp.exp(prior_log)[:, None, None] * init_state
    entering = enter_state + jnp.exp(enter_log)[:, :, None, None] * incoming[None]
    inter_out = jnp.exp(cumulative)[..., None] * jnp.einsum(
        "chpn,ctn->cthp", entering, queries, precision=PRECISE
    )
    mixed_out = (intra_out + inter_out + skip[None, None, :, None] * inputs).reshape(
        token_count, channels
    )
    mixer = (mixed_out * jax.nn.silu(z_gate.astype(jnp.float32))).astype(jnp.bfloat16)
    token_mix = lax.all_to_all(mixer, "exp", split_axis=0, concat_axis=1, tiled=True)
    stream = (residual.astype(jnp.float32) + token_mix.astype(jnp.float32)).astype(jnp.bfloat16)
    widened = stream.astype(jnp.float32)
    normed = (
        widened
        * lax.rsqrt(jnp.mean(widened * widened, axis=-1, keepdims=True) + 1e-06)
        * norm_gain[None, :]
    ).astype(jnp.bfloat16)
    rows_here = residual.shape[0]
    owners = lax.axis_size("exp")
    local_experts = w_gate.shape[0]
    experts = owners * local_experts
    capacity = max(2, 2 * rows_here // experts + 1)
    width = residual.shape[1]
    chosen = expert_ids.reshape(-1)
    onehot = (chosen[:, None] == jnp.arange(experts)[None, :]).astype(jnp.int32)
    slot_index = jnp.sum((jnp.cumsum(onehot, axis=0) - onehot) * onehot, axis=1)
    target = slot_index * experts + chosen
    placing = (target[None, :] == jnp.arange(experts * capacity)[:, None]).astype(jnp.bfloat16)
    pair_rows = jnp.repeat(normed, 2, axis=0)
    outgoing = jnp.dot(placing, pair_rows, preferred_element_type=jnp.float32).astype(jnp.bfloat16)
    outgoing = outgoing.reshape(capacity, experts, width)
    arrived = lax.all_to_all(outgoing, "exp", split_axis=1, concat_axis=1, tiled=True)
    pieces = []
    for first, last in ((0, 1), (1, capacity)):
        chunk = arrived[first:last].reshape((last - first) * experts, width)
        segment = lax.all_gather(chunk, "seq", axis=0, tiled=True)
        gate_proj = jnp.dot(segment, w_gate[0], preferred_element_type=jnp.float32)
        up_proj = jnp.dot(segment, w_up[0], preferred_element_type=jnp.float32)
        active = (jax.nn.silu(gate_proj) * up_proj).astype(jnp.bfloat16)
        partial_value = jnp.dot(active, w_down[0], preferred_element_type=jnp.float32)
        pieces.append(
            lax.psum_scatter(
                partial_value.astype(jnp.bfloat16), "seq", scatter_dimension=0, tiled=True
            )
        )
    summed = jnp.concatenate(pieces, axis=0).reshape(capacity, experts, width)
    returned = lax.all_to_all(summed, "exp", split_axis=1, concat_axis=1, tiled=True)
    results = returned.reshape(experts * capacity, width)
    picked = results[target].astype(jnp.float32).reshape(rows_here, 2, width)
    mixture = jnp.sum(picked * gate_weights[:, :, None], axis=1)
    return (widened + mixture).astype(jnp.bfloat16)


def solution(mesh):
    return jax.shard_map(
        on_device,
        mesh=mesh,
        in_specs=(
            P("seq", "exp"),
            P("seq", "exp"),
            P("seq", None),
            P("seq", None),
            P("seq", "exp"),
            P("exp"),
            P("exp"),
            P("exp", None, None),
            P(("seq", "exp"), None),
            P(),
            P(("seq", "exp"), None),
            P(("seq", "exp"), None),
            P("exp", None, "seq"),
            P("exp", None, "seq"),
            P("exp", "seq", None),
        ),
        out_specs=P(("seq", "exp"), None),
        check_vma=False,
    )
```

profile of v0, /device:TPU:1, one launch (start us, length us, event | category | flops | bytes accessed | tf_op | source)
XLA Modules:
  0.0 493.9 jit_solution(8506652656855577056)
XLA Ops:
  13.0 4.0 collective-permute-start.3
  17.0 3.1 collective-permute-start
  20.1 1.9 collective-permute-done
  22.1 5.6 %collective-permute-start.4 = (f32[8,64,128]{2,1,0:T(8,128)S(1)}, f32[8,64,128]{2,1,0:T(8,128)S(1)}, u32[]{:S(2)}, u32[]{:S(2)}) collective-permute-start(f32[8,64,128]{2,1,0:T(8,128)S(1)} %multiply_add_fusion.3), channel_id=1, source_target_pairs={{0,32},{16,48},{32,64},{48,80},{64,96},{80,112},{96,128},{112,144}... | collective-permute-start | bytes 786440 | tf_op jit(solution)/shard_map/ppermute | solution.py:17
  27.7 3.9 collective-permute-done.4
  31.7 7.2 %collective-permute-start.5 = (f32[8,64,128]{2,1,0:T(8,128)S(1)}, f32[8,64,128]{2,1,0:T(8,128)S(1)}, u32[]{:S(2)}, u32[]{:S(2)}) collective-permute-start(f32[8,64,128]{2,1,0:T(8,128)S(1)} %multiply_add_fusion.2), channel_id=1, source_target_pairs={{0,64},{16,80},{32,96},{48,112},{64,128},{80,144},{96,160},{112,17... | collective-permute-start | bytes 786440 | tf_op jit(solution)/shard_map/ppermute | solution.py:17
  44.3 9.5 %collective-permute-start.6 = (f32[8,64,128]{2,1,0:T(8,128)}, f32[8,64,128]{2,1,0:T(8,128)}, u32[]{:S(2)}, u32[]{:S(2)}) collective-permute-start(f32[8,64,128]{2,1,0:T(8,128)} %multiply_add_fusion.1), channel_id=1, source_target_pairs={{0,128},{16,144},{32,160},{48,176},{64,192},{80,208},{96,224},{112... | collective-permute-start | bytes 786440 | tf_op jit(solution)/shard_map/ppermute | solution.py:17
  60.2 3.3 collective-permute-start.7
  67.6 2.2 fusion.17
  71.3 14.3 %all-to-all-start = ((bf16[16,16,512]{2,1,0:T(8,128)(2,1)}), bf16[16,16,512]{2,1,0:T(8,128)(2,1)S(1)}, u32[]{:S(2)}, u32[]{:S(2)}) async-start(bf16[16,16,512]{2,1,0:T(8,128)(2,1)} %bitcast.10), calls=%async_computation | async-start | bytes 524288 | tf_op jit(solution)/shard_map/all_to_all | solution.py:88
  86.0 11.3 %all-to-all-done = bf16[16,16,512]{2,1,0:T(8,128)(2,1)S(1)} async-done(((bf16[16,16,512]{2,1,0:T(8,128)(2,1)}), bf16[16,16,512]{2,1,0:T(8,128)(2,1)S(1)}, u32[]{:S(2)}, u32[]{:S(2)}) %all-to-all-start) | async-done | bytes 262176 | tf_op jit(solution)/shard_map/all_to_all | solution.py:88
  99.4 31.2 %all_to_all.23 = bf16[3,16,8192]{2,0,1:T(4,128)(2,1)S(1)} all-to-all(bf16[3,16,8192]{2,0,1:T(4,128)(2,1)S(1)} %copy.99), channel_id=1, replica_groups=mesh['seq'=16,'exp'=16] {'exp'}, dimensions={1} | all-to-all | bytes 1572864 | tf_op jit(solution)/shard_map/all_to_all | solution.py:110
  134.1 49.5 %all-gather.6.cloned.1.call-done = bf16[1,256,8192]{2,1,0:T(8,128)(2,1)} async-done(((bf16[1,16,8192]{2,1,0:T(8,128)(2,1)}), bf16[1,256,8192]{2,1,0:T(8,128)(2,1)}) %all-gather.6.cloned.1.call-update) | async-done | bytes 4194320 | tf_op jit(solution)/shard_map/all_gather | solution.py:114
  183.6 4.1 fusion.6
  187.7 7.3 %convolution_convert_fusion.1 = bf16[256,8192]{1,0:T(8,128)(2,1)} fusion(bf16[1,128,8192]{2,1,0:T(8,128)(2,1)S(1)} %copy-done, bf16[1,8192,128]{2,1,0:T(8,128)(2,1)} %param.30, bf16[1,256,8192]{2,1,0:T(8,128)(2,1)} %all-gather.6.cloned.1.call-done, f32[256,128]{1,0:T(8,128)S(1)} %fusion.6), kind=kOutput, calls=%fused_computation.10 | convolution fusion | flops 1076035584 | bytes 12713984 | tf_op jit(solution)/shard_map/dot_general | solution.py:118
  195.1 66.5 %all-gather.4.cloned.1.call-done = bf16[512,8192]{1,0:T(8,128)(2,1)} async-done(((bf16[32,8192]{1,0:T(8,128)(2,1)}), bf16[512,8192]{1,0:T(8,128)(2,1)}) %all-gather.4.cloned.1.call-update) | async-done | bytes 8388624 | tf_op jit(solution)/shard_map/all_gather | solution.py:114
  261.6 6.4 %fusion.13 = f32[512,128]{1,0:T(8,128)S(1)} fusion(bf16[512,8192]{1,0:T(8,128)(2,1)} %all-gather.4.cloned.1.call-done, bf16[1,8192,128]{2,1,0:T(8,128)(2,1)} %param.29), kind=kOutput, calls=%fused_computation.21 | convolution fusion | flops 1073741824 | bytes 10747904 | tf_op jit(solution)/shard_map/dot_general | solution.py:115
  268.6 2.3 fusion.22
  270.9 5.6 %convolution_convert_fusion = bf16[512,8192]{1,0:T(8,128)(2,1)} fusion(bf16[512,128]{1,0:T(8,128)(2,1)S(1)} %fusion.22, bf16[1,128,8192]{2,1,0:T(8,128)(2,1)S(1)} %copy-done), kind=kOutput, calls=%fused_computation.9 | convolution fusion | flops 1077936128 | bytes 10616832 | tf_op jit(solution)/shard_map/dot_general | solution.py:118
  276.5 69.4 %reduce-scatter.3.cloned.1.call-done = bf16[16,8192]{1,0:T(8,128)(2,1)} async-done(((bf16[256,8192]{1,0:T(8,128)(2,1)}), bf16[16,8192]{1,0:T(8,128)(2,1)}) %reduce-scatter.3.cloned.1.call-update) | async-done | bytes 262160 | tf_op jit(solution)/shard_map/reduce_scatter | solution.py:120
  345.9 94.2 %reduce-scatter.5.cloned.1.call-done = bf16[32,8192]{1,0:T(8,128)(2,1)} async-done(((bf16[512,8192]{1,0:T(8,128)(2,1)}), bf16[32,8192]{1,0:T(8,128)(2,1)}) %reduce-scatter.5.cloned.1.call-update) | async-done | bytes 524304 | tf_op jit(solution)/shard_map/reduce_scatter | solution.py:120
  443.0 9.0 %all-to-all-start.2 = ((bf16[3,16,8192]{2,0,1:T(4,128)(2,1)}), bf16[3,16,8192]{2,0,1:T(4,128)(2,1)}, u32[]{:S(2)}, u32[]{:S(2)}) async-start(bf16[3,16,8192]{2,0,1:T(4,128)(2,1)} %copy.102), calls=%async_computation.4 | async-start | bytes 2097152 | tf_op jit(solution)/shard_map/all_to_all | solution.py:125
  452.2 27.8 %all-to-all-done.2 = bf16[3,16,8192]{2,0,1:T(4,128)(2,1)} async-done(((bf16[3,16,8192]{2,0,1:T(4,128)(2,1)}), bf16[3,16,8192]{2,0,1:T(4,128)(2,1)}, u32[]{:S(2)}, u32[]{:S(2)}) %all-to-all-start.2) | async-done | bytes 786464 | tf_op jit(solution)/shard_map/all_to_all | solution.py:125
  480.0 1.8 copy.103
  (106 shorter events, 40.5 us)
Async XLA Ops:
  6.5 181.2 %copy-start = (bf16[1,128,8192]{2,1,0:T(8,128)(2,1)S(1)}, bf16[1,128,8192]{2,1,0:T(8,128)(2,1)}, u32[]{:S(2)}) copy-start(bf16[1,128,8192]{2,1,0:T(8,128)(2,1)} %param.31) | copy-start | bytes 6291460
  6.5 4.3 copy-start.3
  13.0 9.0 %collective-permute-start.3 = (f32[8,64,128]{2,1,0:T(8,128)S(1)}, f32[8,64,128]{2,1,0:T(8,128)S(1)}, u32[]{:S(2)}, u32[]{:S(2)}) collective-permute-start(f32[8,64,128]{2,1,0:T(8,128)S(1)} %get-tuple-element.48), channel_id=1, source_target_pairs={{0,16},{16,32},{32,48},{48,64},{64,80},{80,96},{96,112},{112,128},... | collective-permute-start | bytes 786440 | tf_op jit(solution)/shard_map/ppermute | solution.py:17
  17.0 5.0 %collective-permute-start = (f32[8]{0:T(128)S(1)}, f32[8]{0:T(128)S(1)}, u32[]{:S(2)}, u32[]{:S(2)}) collective-permute-start(f32[8]{0:T(128)S(1)} %get-tuple-element.47), channel_id=1, source_target_pairs={{0,16},{16,32},{32,48},{48,64},{64,80},{80,96},{96,112},{112,128},... | collective-permute-start | bytes 104 | tf_op jit(solution)/shard_map/ppermute | solution.py:17
  22.0 9.7 %copy-start.6 = (f32[8]{0:T(128)}, f32[8]{0:T(128)S(1)}, u32[]{:S(2)}) copy-start(f32[8]{0:T(128)S(1)} %collective-permute-done) | copy-start | bytes 100
  22.1 9.6 %collective-permute-start.4 = (f32[8,64,128]{2,1,0:T(8,128)S(1)}, f32[8,64,128]{2,1,0:T(8,128)S(1)}, u32[]{:S(2)}, u32[]{:S(2)}) collective-permute-start(f32[8,64,128]{2,1,0:T(8,128)S(1)} %multiply_add_fusion.3), channel_id=1, source_target_pairs={{0,32},{16,48},{32,64},{48,80},{64,96},{80,112},{96,128},{112,144}... | collective-permute-start | bytes 786440 | tf_op jit(solution)/shard_map/ppermute | solution.py:17
  31.7 11.8 %collective-permute-start.5 = (f32[8,64,128]{2,1,0:T(8,128)S(1)}, f32[8,64,128]{2,1,0:T(8,128)S(1)}, u32[]{:S(2)}, u32[]{:S(2)}) collective-permute-start(f32[8,64,128]{2,1,0:T(8,128)S(1)} %multiply_add_fusion.2), channel_id=1, source_target_pairs={{0,64},{16,80},{32,96},{48,112},{64,128},{80,144},{96,160},{112,17... | collective-permute-start | bytes 786440 | tf_op jit(solution)/shard_map/ppermute | solution.py:17
  40.6 2.3 collective-permute-start.1
  43.0 0.6 copy-start.7
  44.3 20.5 %collective-permute-start.6 = (f32[8,64,128]{2,1,0:T(8,128)}, f32[8,64,128]{2,1,0:T(8,128)}, u32[]{:S(2)}, u32[]{:S(2)}) collective-permute-start(f32[8,64,128]{2,1,0:T(8,128)} %multiply_add_fusion.1), channel_id=1, source_target_pairs={{0,128},{16,144},{32,160},{48,176},{64,192},{80,208},{96,224},{112... | collective-permute-start | bytes 786440 | tf_op jit(solution)/shard_map/ppermute | solution.py:17
  54.6 13.0 %copy-start.5 = (pred[128,128]{1,0:T(8,128)(4,1)S(1)}, pred[128,128]{1,0:T(8,128)(4,1)}, u32[]{:S(2)}) copy-start(pred[128,128]{1,0:T(8,128)(4,1)} %iota_compare_fusion) | copy-start | bytes 49156
  57.5 2.1 collective-permute-start.2
  60.2 4.0 collective-permute-start.7
  70.2 27.2 %copy-start.2 = (bf16[16,8192]{1,0:T(8,128)(2,1)S(1)}, bf16[16,8192]{1,0:T(8,128)(2,1)}, u32[]{:S(2)}) copy-start(bf16[16,8192]{1,0:T(8,128)(2,1)} %param.25) | copy-start | bytes 786436
  70.4 27.2 %copy-start.4 = (f32[8192]{0:T(1024)S(1)}, f32[8192]{0:T(1024)}, u32[]{:S(2)}) copy-start(f32[8192]{0:T(1024)} %param.26) | copy-start | bytes 98308
  71.3 26.0 %all-to-all-start = ((bf16[16,16,512]{2,1,0:T(8,128)(2,1)}), bf16[16,16,512]{2,1,0:T(8,128)(2,1)S(1)}, u32[]{:S(2)}, u32[]{:S(2)}) async-start(bf16[16,16,512]{2,1,0:T(8,128)(2,1)} %bitcast.10), calls=%async_computation | async-start | bytes 524288 | tf_op jit(solution)/shard_map/all_to_all | solution.py:88
  85.6 98.0 %all-gather.6.cloned.1.call-start = ((), (), s32[]{:S(2)}) async-start(), calls=%async_computation.8 | async-start | bytes 4456448 | tf_op jit(solution)/shard_map/all_gather | solution.py:114
  132.1 129.5 %all-gather.4.cloned.1.call-start = ((), (), s32[]{:S(2)}) async-start(), calls=%async_computation.6 | async-start | bytes 8912896 | tf_op jit(solution)/shard_map/all_gather | solution.py:114
  133.9 212.1 %reduce-scatter.3.cloned.1.call-start = ((), (), s32[]{:S(2)}) async-start(), calls=%async_computation.5 | async-start | bytes 4456448 | tf_op jit(solution)/shard_map/reduce_scatter | solution.py:120
  195.0 245.2 %reduce-scatter.5.cloned.1.call-start = ((), (), s32[]{:S(2)}) async-start(), calls=%async_computation.7 | async-start | bytes 8912896 | tf_op jit(solution)/shard_map/reduce_scatter | solution.py:120
  261.6 6.5 %copy-start.1 = (bf16[1,8192,128]{2,1,0:T(8,128)(2,1)S(1)}, bf16[1,8192,128]{2,1,0:T(8,128)(2,1)}, u32[]{:S(2)}) copy-start(bf16[1,8192,128]{2,1,0:T(8,128)(2,1)} %param.30) | copy-start | bytes 6291460
  261.6 7.0 %copy-start.9 = (bf16[512,8192]{1,0:T(8,128)(2,1)S(1)}, bf16[512,8192]{1,0:T(8,128)(2,1)}, u32[]{:S(2)}) copy-start(bf16[512,8192]{1,0:T(8,128)(2,1)} %all-gather.4.cloned.1.call-done) | copy-start | bytes 25165828
  441.4 10.7 %copy-start.8 = (f32[16,2]{0,1:T(2,128)S(1)}, f32[16,2]{0,1:T(2,128)}, u32[]{:S(2)}) copy-start(f32[16,2]{0,1:T(2,128)} %param.28) | copy-start | bytes 388
  443.0 37.0 %all-to-all-start.2 = ((bf16[3,16,8192]{2,0,1:T(4,128)(2,1)}), bf16[3,16,8192]{2,0,1:T(4,128)(2,1)}, u32[]{:S(2)}, u32[]{:S(2)}) async-start(bf16[3,16,8192]{2,0,1:T(4,128)(2,1)} %copy.102), calls=%async_computation.4 | async-start | bytes 2097152 | tf_op jit(solution)/shard_map/all_to_all | solution.py:125
Sparse Core Ops, SparseCore 0:
  132.2 51.3 all-gather.5
  186.0 75.4 all-gather.3
  265.2 80.6 reduce-scatter.2
  350.0 90.1 reduce-scatter.4
where the time goes:
time: 495 us; the launch traced here: 494 us
  waiting for transfers between devices  327 us (66%)
  starting transfers between devices  59.2 us (12%)
  matrix products  31.9 us (6%)
  blocking collectives  31.2 us (6%)
  local copies, waits for them, and re-layouts  18.1 us (4%)
  between operations  13.5 us (3%)
  other arithmetic  13 us (3%)
    reduce_scatter x2, waiting for transfers between devices, on_device(): lax.psum_scatter(partial_value.astype(jnp.bfloat16), 'seq', scatter_dimen...  164 us
    all_gather x2, waiting for transfers between devices, on_device(): segment = lax.all_gather(chunk, 'seq', axis=0, tiled=True)  116 us
    ppermute x8, starting transfers between devices, exclusive_scan(): got = (lax.ppermute(inc[0], axis, pairs), lax.ppermute(inc[1], axis, pairs))  35.6 us
    all_to_all x1, blocking collectives, on_device(): lax.all_to_all(outgoing, 'exp', split_axis=1, concat_axis=1, tiled=True)  31.2 us
    all_to_all x1, waiting for transfers between devices, on_device(): lax.all_to_all(summed, 'exp', split_axis=1, concat_axis=1, tiled=True)  27.8 us
    all_to_all x1, starting transfers between devices, on_device(): lax.all_to_all(mixer, 'exp', split_axis=0, concat_axis=1, tiled=True)  14.3 us
    dot_general x2, matrix products, on_device(): jnp.dot(active, w_down[0], preferred_element_type=jnp.float32)  12.8 us
    all_to_all x1, waiting for transfers between devices, on_device(): lax.all_to_all(mixer, 'exp', split_axis=0, concat_axis=1, tiled=True)  11.3 us
  transfers between devices with their start and end apart: 14, of which 11 were waited for; matrix products, arithmetic and copies ran while one was open for 7% of the time, Pallas kernels for 0%

commit v1 on v0

--- a/solution.py
+++ b/solution.py
@@ -111,7 +111,10 @@
     pieces = []
     for first, last in ((0, 1), (1, capacity)):
         chunk = arrived[first:last].reshape((last - first) * experts, width)
-        segment = lax.all_gather(chunk, "seq", axis=0, tiled=True)
+        size = lax.axis_size("seq")
+        parts = jnp.stack([chunk for _ in range(size)])
+        parts = lax.all_to_all(parts, "seq", split_axis=0, concat_axis=0)
+        segment = jnp.concatenate(parts, axis=0)
         gate_proj = jnp.dot(segment, w_gate[0], preferred_element_type=jnp.float32)
         up_proj = jnp.dot(segment, w_up[0], preferred_element_type=jnp.float32)
         active = (jax.nn.silu(gate_proj) * up_proj).astype(jnp.bfloat16)

time: 495 us -> 531 us (1.073)
  waiting for transfers between devices: 327 us -> 345 us
  starting transfers between devices: 59.2 us -> 68.4 us
    all_to_all x0 -> x2, waiting for transfers between devices: none -> 187 us  [on_device(): parts = lax.all_to_all(parts, 'seq', split_axis=0, concat_axis=0)]
    all_gather x2 -> x0, waiting for transfers between devices: 116 us -> none  [on_device(): segment = lax.all_gather(chunk, 'seq', axis=0, tiled=True)]
    reduce_scatter x2, waiting for transfers between devices: 164 us -> 110 us  [on_device(): lax.psum_scatter(partial_value.astype(jnp.bfloat16), 'seq', scatter_dimen...]
    all_to_all x0 -> x2, starting transfers between devices: none -> 9.64 us  [on_device(): parts = lax.all_to_all(parts, 'seq', split_axis=0, concat_axis=0)]
    another operation x0 -> x2, local copies, waits for them, and re-layouts: none -> 6.7 us  [on_device(): parts = jnp.stack([chunk for _ in range(size)])]
where the time goes in v1:
time: 531 us; the launch traced here: 530 us
  waiting for transfers between devices  345 us (65%)
  starting transfers between devices  68.4 us (13%)
  matrix products  35.5 us (7%)
  blocking collectives  31.2 us (6%)
  local copies, waits for them, and re-layouts  22.8 us (4%)
  between operations  13.8 us (3%)
  other arithmetic  13.1 us (2%)
    all_to_all x2, waiting for transfers between devices, on_device(): parts = lax.all_to_all(parts, 'seq', split_axis=0, concat_axis=0)  187 us
    reduce_scatter x2, waiting for transfers between devices, on_device(): lax.psum_scatter(partial_value.astype(jnp.bfloat16), 'seq', scatter_dimen...  110 us
    ppermute x8, starting transfers between devices, exclusive_scan(): got = (lax.ppermute(inc[0], axis, pairs), lax.ppermute(inc[1], axis, pairs))  35.6 us
    all_to_all x1, blocking collectives, on_device(): lax.all_to_all(outgoing, 'exp', split_axis=1, concat_axis=1, tiled=True)  31.2 us
    all_to_all x1, waiting for transfers between devices, on_device(): lax.all_to_all(summed, 'exp', split_axis=1, concat_axis=1, tiled=True)  27.8 us
    all_to_all x1, starting transfers between devices, on_device(): lax.all_to_all(mixer, 'exp', split_axis=0, concat_axis=1, tiled=True)  14 us
    dot_general x2, matrix products, on_device(): jnp.dot(active, w_down[0], preferred_element_type=jnp.float32)  12.8 us
    all_to_all x1, waiting for transfers between devices, on_device(): lax.all_to_all(mixer, 'exp', split_axis=0, concat_axis=1, tiled=True)  11.4 us
  transfers between devices with their start and end apart: 14, of which 11 were waited for; matrix products, arithmetic and copies ran while one was open for 7% of the time, Pallas kernels for 0%

profile of v1, /device:TPU:1, one launch (start us, length us, event | category | flops | bytes accessed | tf_op | source)
XLA Modules:
  0.0 529.6 jit_solution(6539703627572766895)
XLA Ops:
  13.0 4.0 collective-permute-start.3
  17.0 3.1 collective-permute-start
  22.1 5.6 %collective-permute-start.4 = (f32[8,64,128]{2,1,0:T(8,128)S(1)}, f32[8,64,128]{2,1,0:T(8,128)S(1)}, u32[]{:S(2)}, u32[]{:S(2)}) collective-permute-start(f32[8,64,128]{2,1,0:T(8,128)S(1)} %multiply_add_fusion.3), channel_id=1, source_target_pairs={{0,32},{16,48},{32,64},{48,80},{64,96},{80,112},{96,128},{112,144}... | collective-permute-start | bytes 786440 | tf_op jit(solution)/shard_map/ppermute | solution.py:17
  27.7 3.9 collective-permute-done.4
  31.7 7.2 %collective-permute-start.5 = (f32[8,64,128]{2,1,0:T(8,128)S(1)}, f32[8,64,128]{2,1,0:T(8,128)S(1)}, u32[]{:S(2)}, u32[]{:S(2)}) collective-permute-start(f32[8,64,128]{2,1,0:T(8,128)S(1)} %multiply_add_fusion.2), channel_id=1, source_target_pairs={{0,64},{16,80},{32,96},{48,112},{64,128},{80,144},{96,160},{112,17... | collective-permute-start | bytes 786440 | tf_op jit(solution)/shard_map/ppermute | solution.py:17
  44.4 9.5 %collective-permute-start.6 = (f32[8,64,128]{2,1,0:T(8,128)}, f32[8,64,128]{2,1,0:T(8,128)}, u32[]{:S(2)}, u32[]{:S(2)}) collective-permute-start(f32[8,64,128]{2,1,0:T(8,128)} %multiply_add_fusion.1), channel_id=1, source_target_pairs={{0,128},{16,144},{32,160},{48,176},{64,192},{80,208},{96,224},{112... | collective-permute-start | bytes 786440 | tf_op jit(solution)/shard_map/ppermute | solution.py:17
  60.4 3.3 collective-permute-start.7
  71.4 14.0 %all-to-all-start = ((bf16[16,16,512]{2,1,0:T(8,128)(2,1)}), bf16[16,16,512]{2,1,0:T(8,128)(2,1)S(1)}, u32[]{:S(2)}, u32[]{:S(2)}) async-start(bf16[16,16,512]{2,1,0:T(8,128)(2,1)} %bitcast.10), calls=%async_computation | async-start | bytes 524288 | tf_op jit(solution)/shard_map/all_to_all | solution.py:88
  85.8 11.4 %all-to-all-done = bf16[16,16,512]{2,1,0:T(8,128)(2,1)S(1)} async-done(((bf16[16,16,512]{2,1,0:T(8,128)(2,1)}), bf16[16,16,512]{2,1,0:T(8,128)(2,1)S(1)}, u32[]{:S(2)}, u32[]{:S(2)}) %all-to-all-start) | async-done | bytes 262176 | tf_op jit(solution)/shard_map/all_to_all | solution.py:88
  99.3 31.2 %all_to_all.33 = bf16[3,16,8192]{2,0,1:T(4,128)(2,1)S(1)} all-to-all(bf16[3,16,8192]{2,0,1:T(4,128)(2,1)S(1)} %copy.99), channel_id=1, replica_groups=mesh['seq'=16,'exp'=16] {'exp'}, dimensions={1} | all-to-all | bytes 1572864 | tf_op jit(solution)/shard_map/all_to_all | solution.py:110
  133.7 4.9 all-to-all-start.2
  139.5 63.9 %all-to-all-done.2 = bf16[16,16,8192]{2,1,0:T(8,128)(2,1)} async-done(((bf16[16,16,8192]{2,1,0:T(8,128)(2,1)}), bf16[16,16,8192]{2,1,0:T(8,128)(2,1)}, u32[]{:S(2)}, u32[]{:S(2)}) %all-to-all-start.2) | async-done | bytes 4194336 | tf_op jit(solution)/shard_map/all_to_all | solution.py:116
  203.4 4.3 stack.7
  207.7 4.7 all-to-all-start.3
  212.6 4.1 fusion.12
  216.8 7.2 %convolution_convert_fusion.1 = bf16[256,8192]{1,0:T(8,128)(2,1)} fusion(bf16[1,128,8192]{2,1,0:T(8,128)(2,1)S(1)} %copy-done, bf16[256,8192]{1,0:T(8,128)(2,1)} %bitcast.14, bf16[1,8192,128]{2,1,0:T(8,128)(2,1)} %param.30, f32[256,128]{1,0:T(8,128)S(1)} %fusion.12), kind=kOutput, calls=%fused_computation.10 | convolution fusion | flops 1076035584 | bytes 12713984 | tf_op jit(solution)/shard_map/dot_general | solution.py:121
  224.1 123.6 %all-to-all-done.3 = bf16[16,32,8192]{2,1,0:T(8,128)(2,1)} async-done(((bf16[16,32,8192]{2,1,0:T(8,128)(2,1)}), bf16[16,32,8192]{2,1,0:T(8,128)(2,1)}, u32[]{:S(2)}, u32[]{:S(2)}) %all-to-all-start.3) | async-done | bytes 8388640 | tf_op jit(solution)/shard_map/all_to_all | solution.py:116
  347.7 6.6 %fusion.10 = f32[512,128]{1,0:T(8,128)S(1)} fusion(bf16[512,8192]{1,0:T(8,128)(2,1)} %bitcast.19, bf16[1,8192,128]{2,1,0:T(8,128)(2,1)} %param.29), kind=kOutput, calls=%fused_computation.18 | convolution fusion | flops 1073741824 | bytes 10747904 | tf_op jit(solution)/shard_map/dot_general | solution.py:118
  354.3 5.8 %fusion.20 = bf16[512,128]{1,0:T(8,128)(2,1)S(1)} fusion(bf16[512,8192]{1,0:T(8,128)(2,1)} %bitcast.19, bf16[1,8192,128]{2,1,0:T(8,128)(2,1)S(1)} %copy-done.1, f32[512,128]{1,0:T(8,128)S(1)} %fusion.10), kind=kOutput, calls=%fused_computation.28 | convolution fusion | flops 1074135040 | bytes 10878976 | tf_op jit(solution)/shard_map/dot_general | solution.py:119
  360.1 5.6 %convolution_convert_fusion = bf16[512,8192]{1,0:T(8,128)(2,1)} fusion(bf16[512,128]{1,0:T(8,128)(2,1)S(1)} %fusion.20, bf16[1,128,8192]{2,1,0:T(8,128)(2,1)S(1)} %copy-done), kind=kOutput, calls=%fused_computation.9 | convolution fusion | flops 1077936128 | bytes 10616832 | tf_op jit(solution)/shard_map/dot_general | solution.py:121
  365.7 15.6 %reduce-scatter.3.cloned.1.call-done = bf16[16,8192]{1,0:T(8,128)(2,1)} async-done(((bf16[256,8192]{1,0:T(8,128)(2,1)}), bf16[16,8192]{1,0:T(8,128)(2,1)}) %reduce-scatter.3.cloned.1.call-update) | async-done | bytes 262160 | tf_op jit(solution)/shard_map/reduce_scatter | solution.py:123
  381.3 94.3 %reduce-scatter.5.cloned.1.call-done = bf16[32,8192]{1,0:T(8,128)(2,1)} async-done(((bf16[512,8192]{1,0:T(8,128)(2,1)}), bf16[32,8192]{1,0:T(8,128)(2,1)}) %reduce-scatter.5.cloned.1.call-update) | async-done | bytes 524304 | tf_op jit(solution)/shard_map/reduce_scatter | solution.py:123
  478.5 8.9 %all-to-all-start.4 = ((bf16[3,16,8192]{2,0,1:T(4,128)(2,1)}), bf16[3,16,8192]{2,0,1:T(4,128)(2,1)}, u32[]{:S(2)}, u32[]{:S(2)}) async-start(bf16[3,16,8192]{2,0,1:T(4,128)(2,1)} %copy.102), calls=%async_computation.6 | async-start | bytes 2097152 | tf_op jit(solution)/shard_map/all_to_all | solution.py:128
  487.5 27.8 %all-to-all-done.4 = bf16[3,16,8192]{2,0,1:T(4,128)(2,1)} async-done(((bf16[3,16,8192]{2,0,1:T(4,128)(2,1)}), bf16[3,16,8192]{2,0,1:T(4,128)(2,1)}, u32[]{:S(2)}, u32[]{:S(2)}) %all-to-all-start.4) | async-done | bytes 786464 | tf_op jit(solution)/shard_map/all_to_all | solution.py:128
  (104 shorter events, 46.9 us)
Async XLA Ops:
  6.5 210.2 %copy-start = (bf16[1,128,8192]{2,1,0:T(8,128)(2,1)S(1)}, bf16[1,128,8192]{2,1,0:T(8,128)(2,1)}, u32[]{:S(2)}) copy-start(bf16[1,128,8192]{2,1,0:T(8,128)(2,1)} %param.31) | copy-start | bytes 6291460
  6.5 4.3 copy-start.3
  13.0 9.0 %collective-permute-start.3 = (f32[8,64,128]{2,1,0:T(8,128)S(1)}, f32[8,64,128]{2,1,0:T(8,128)S(1)}, u32[]{:S(2)}, u32[]{:S(2)}) collective-permute-start(f32[8,64,128]{2,1,0:T(8,128)S(1)} %get-tuple-element.48), channel_id=1, source_target_pairs={{0,16},{16,32},{32,48},{48,64},{64,80},{80,96},{96,112},{112,128},... | collective-permute-start | bytes 786440 | tf_op jit(solution)/shard_map/ppermute | solution.py:17
  17.0 5.0 collective-permute-start
  21.9 9.7 %copy-start.6 = (f32[8]{0:T(128)}, f32[8]{0:T(128)S(1)}, u32[]{:S(2)}) copy-start(f32[8]{0:T(128)S(1)} %collective-permute-done) | copy-start | bytes 100
  22.1 9.6 %collective-permute-start.4 = (f32[8,64,128]{2,1,0:T(8,128)S(1)}, f32[8,64,128]{2,1,0:T(8,128)S(1)}, u32[]{:S(2)}, u32[]{:S(2)}) collective-permute-start(f32[8,64,128]{2,1,0:T(8,128)S(1)} %multiply_add_fusion.3), channel_id=1, source_target_pairs={{0,32},{16,48},{32,64},{48,80},{64,96},{80,112},{96,128},{112,144}... | collective-permute-start | bytes 786440 | tf_op jit(solution)/shard_map/ppermute | solution.py:17
  31.7 11.8 %collective-permute-start.5 = (f32[8,64,128]{2,1,0:T(8,128)S(1)}, f32[8,64,128]{2,1,0:T(8,128)S(1)}, u32[]{:S(2)}, u32[]{:S(2)}) collective-permute-start(f32[8,64,128]{2,1,0:T(8,128)S(1)} %multiply_add_fusion.2), channel_id=1, source_target_pairs={{0,64},{16,80},{32,96},{48,112},{64,128},{80,144},{96,160},{112,17... | collective-permute-start | bytes 786440 | tf_op jit(solution)/shard_map/ppermute | solution.py:17
  40.6 2.3 collective-permute-start.1
  43.0 10.9 %copy-start.7 = (f32[8]{0:T(128)}, f32[8]{0:T(128)S(1)}, u32[]{:S(2)}) copy-start(f32[8]{0:T(128)S(1)} %collective-permute-done.1) | copy-start | bytes 100
  44.4 20.7 %collective-permute-start.6 = (f32[8,64,128]{2,1,0:T(8,128)}, f32[8,64,128]{2,1,0:T(8,128)}, u32[]{:S(2)}, u32[]{:S(2)}) collective-permute-start(f32[8,64,128]{2,1,0:T(8,128)} %multiply_add_fusion.1), channel_id=1, source_target_pairs={{0,128},{16,144},{32,160},{48,176},{64,192},{80,208},{96,224},{112... | collective-permute-start | bytes 786440 | tf_op jit(solution)/shard_map/ppermute | solution.py:17
  54.6 13.2 %copy-start.5 = (pred[128,128]{1,0:T(8,128)(4,1)S(1)}, pred[128,128]{1,0:T(8,128)(4,1)}, u32[]{:S(2)}) copy-start(pred[128,128]{1,0:T(8,128)(4,1)} %iota_compare_fusion) | copy-start | bytes 49156
  57.5 2.2 collective-permute-start.2
  60.4 4.0 collective-permute-start.7
  70.4 26.9 %copy-start.2 = (bf16[16,8192]{1,0:T(8,128)(2,1)S(1)}, bf16[16,8192]{1,0:T(8,128)(2,1)}, u32[]{:S(2)}) copy-start(bf16[16,8192]{1,0:T(8,128)(2,1)} %param.25) | copy-start | bytes 786436
  70.6 26.9 %copy-start.4 = (f32[8192]{0:T(1024)S(1)}, f32[8192]{0:T(1024)}, u32[]{:S(2)}) copy-start(f32[8192]{0:T(1024)} %param.26) | copy-start | bytes 98308
  71.4 25.7 %all-to-all-start = ((bf16[16,16,512]{2,1,0:T(8,128)(2,1)}), bf16[16,16,512]{2,1,0:T(8,128)(2,1)S(1)}, u32[]{:S(2)}, u32[]{:S(2)}) async-start(bf16[16,16,512]{2,1,0:T(8,128)(2,1)} %bitcast.10), calls=%async_computation | async-start | bytes 524288 | tf_op jit(solution)/shard_map/all_to_all | solution.py:88
  133.7 69.7 %all-to-all-start.2 = ((bf16[16,16,8192]{2,1,0:T(8,128)(2,1)}), bf16[16,16,8192]{2,1,0:T(8,128)(2,1)}, u32[]{:S(2)}, u32[]{:S(2)}) async-start(bf16[16,16,8192]{2,1,0:T(8,128)(2,1)} %stack.6), calls=%async_computation.2 | async-start | bytes 8388608 | tf_op jit(solution)/shard_map/all_to_all | solution.py:116
  207.7 140.0 %all-to-all-start.3 = ((bf16[16,32,8192]{2,1,0:T(8,128)(2,1)}), bf16[16,32,8192]{2,1,0:T(8,128)(2,1)}, u32[]{:S(2)}, u32[]{:S(2)}) async-start(bf16[16,32,8192]{2,1,0:T(8,128)(2,1)} %stack.7), calls=%async_computation.4 | async-start | bytes 16777216 | tf_op jit(solution)/shard_map/all_to_all | solution.py:116
  212.4 168.9 %reduce-scatter.3.cloned.1.call-start = ((), (), s32[]{:S(2)}) async-start(), calls=%async_computation.7 | async-start | bytes 4456448 | tf_op jit(solution)/shard_map/reduce_scatter | solution.py:123
  224.0 251.6 %reduce-scatter.5.cloned.1.call-start = ((), (), s32[]{:S(2)}) async-start(), calls=%async_computation.8 | async-start | bytes 8912896 | tf_op jit(solution)/shard_map/reduce_scatter | solution.py:123
  347.7 6.6 %copy-start.1 = (bf16[1,8192,128]{2,1,0:T(8,128)(2,1)S(1)}, bf16[1,8192,128]{2,1,0:T(8,128)(2,1)}, u32[]{:S(2)}) copy-start(bf16[1,8192,128]{2,1,0:T(8,128)(2,1)} %param.30) | copy-start | bytes 6291460
  476.8 10.7 %copy-start.8 = (f32[16,2]{0,1:T(2,128)S(1)}, f32[16,2]{0,1:T(2,128)}, u32[]{:S(2)}) copy-start(f32[16,2]{0,1:T(2,128)} %param.28) | copy-start | bytes 388
  478.5 36.9 %all-to-all-start.4 = ((bf16[3,16,8192]{2,0,1:T(4,128)(2,1)}), bf16[3,16,8192]{2,0,1:T(4,128)(2,1)}, u32[]{:S(2)}, u32[]{:S(2)}) async-start(bf16[3,16,8192]{2,0,1:T(4,128)(2,1)} %copy.102), calls=%async_computation.6 | async-start | bytes 2097152 | tf_op jit(solution)/shard_map/all_to_all | solution.py:128
Sparse Core Ops, SparseCore 0:
  224.2 157.1 reduce-scatter.2
  385.5 90.1 reduce-scatter.4
